TPU v7x, 256 devices: a whole 4x4x8 slice. The times are simulated.
256 devices in a mesh: blk: 64 (over x, z, y_hi), col: 4 (over y_lo, core).
Axes of the slice: x: 4, y: 4 (y_hi: 2, y_lo: 2; y = y_hi * 2 + y_lo), z: 8, core: 2. Of those that a mesh axis runs over, the one named last changes fastest.
Arguments:
- points: bfloat16 [32768, 128], P(('blk', 'col')), may hold values from -4.5 to 4.5
- targets: float32 [32768, 32], P(('blk', 'col')), may hold values from -6 to 6
- pivots: int32 [2, 256], replicated, may hold values from 0 to 32767, as said below
Outputs:
- factor: bfloat16 [32768, 512], P(('blk', 'col'))
- solution: float32 [32768, 32], P(('blk', 'col'))
- residual: float32 [32768, 32], P(('blk', 'col'))
Inputs may be any that keep to these rules, and one draw needn't show every extreme that they name: `pivots`: the 512 indices are distinct; 0 and 32767 are among them.
All inputs are finite; a program needn't handle non-finite values.
Results may differ from a plain program's by a relative error of at most 0.012.
Values may be sent and summed in bfloat16 or wider, within the bound.
No kernel may reach another device: no remote copies, remote signals or barrier semaphores. Data moves between devices by JAX's collectives and lax.ppermute only.
A program may use at most 64 MiB of HBM per device.

v0:
```python
import jax
import jax.numpy as jnp
from jax import lax
from jax.sharding import PartitionSpec as P

FEATURES = 128
ITERS = 3
noise_level = 0.5
jitter_level = 0.05
highest = lax.Precision.HIGHEST


def squared_norms(point_rows):
    wide_rows = point_rows.astype(jnp.float32)
    return jnp.sum(wide_rows * wide_rows, axis=1)


def kernel_block(left_rows, left_norms, right_rows, right_norms):
    inner = lax.dot_general(
        left_rows, right_rows, (((1,), (1,)), ((), ())), preferred_element_type=jnp.float32
    )
    distance = left_norms[:, None] + right_norms[None, :] - 2.0 * inner
    return jnp.exp(-2.0 * distance / FEATURES)


def lower_solve(lower_factor, right_rows):
    return jax.scipy.linalg.solve_triangular(lower_factor, right_rows.T, lower=True).T


def build_factor(point_rows, first_pick, second_pick):
    row_norms = squared_norms(point_rows)
    first_norms = squared_norms(first_pick)
    second_norms = squared_norms(second_pick)
    identity_piv = jnp.eye(first_pick.shape[0], dtype=jnp.float32)
    first_chol = jnp.linalg.cholesky(
        kernel_block(first_pick, first_norms, first_pick, first_norms) + jitter_level * identity_piv
    )
    first_coef = lower_solve(
        first_chol, kernel_block(point_rows, row_norms, first_pick, first_norms)
    )
    shared_coef = lower_solve(
        first_chol, kernel_block(second_pick, second_norms, first_pick, first_norms)
    )
    schur_block = (
        kernel_block(second_pick, second_norms, second_pick, second_norms)
        + jitter_level * identity_piv
        - jnp.dot(shared_coef, shared_coef.T, precision=highest)
    )
    second_chol = jnp.linalg.cholesky(schur_block)
    second_cross = kernel_block(point_rows, row_norms, second_pick, second_norms) - jnp.dot(
        first_coef, shared_coef.T, precision=highest
    )
    second_coef = lower_solve(second_chol, second_cross)
    return jnp.concatenate([first_coef, second_coef], axis=1)


def per_device(points, targets, pivots):
    row_count = points.shape[0]
    piv_count = pivots.shape[1]
    shard_index = lax.axis_index("blk") * lax.axis_size("col") + lax.axis_index("col")
    first_row = shard_index * row_count
    flat_pivots = pivots.reshape(-1)
    owned = (
        flat_pivots[:, None] == first_row + jnp.arange(row_count, dtype=jnp.int32)[None, :]
    ).astype(jnp.float32)
    local_pick = jnp.dot(owned, points.astype(jnp.float32), precision=highest)
    picked = lax.psum(local_pick, ("blk", "col")).astype(jnp.bfloat16)
    wide_factor = build_factor(points, picked[:piv_count], picked[piv_count:])
    factor = wide_factor.astype(jnp.bfloat16)
    local_gram = lax.dot_general(
        wide_factor, wide_factor, (((0,), (0,)), ((), ())), precision=highest
    )
    gram = lax.psum(local_gram, ("blk", "col"))
    gram = gram + noise_level * jnp.eye(2 * piv_count, dtype=jnp.float32)
    gram_chol = jnp.linalg.cholesky(gram)

    def precondition(residual_now):
        local_proj = lax.dot_general(
            wide_factor, residual_now, (((0,), (0,)), ((), ())), precision=highest
        )
        projection = lax.psum(local_proj, ("blk", "col"))
        coefficients = jax.scipy.linalg.cho_solve((gram_chol, True), projection)
        scaled = (
            residual_now - jnp.dot(wide_factor, coefficients, precision=highest)
        ) / noise_level
        return (scaled, lax.psum(jnp.sum(residual_now * scaled, axis=0), ("blk", "col")))

    own_block = lax.all_gather(points, "col", axis=0, tiled=True)
    own_norms = squared_norms(own_block)

    def tile_add(total, key_rows, key_norms, direction_rows):
        weights = kernel_block(own_block, own_norms, key_rows, key_norms)
        return total + jnp.dot(weights, direction_rows, precision=highest)

    solution = jnp.zeros_like(targets)
    residual = targets
    direction_now, inner_now = precondition(residual)
    for step_index in range(ITERS):
        empty = jnp.zeros((own_block.shape[0], direction_now.shape[1]), jnp.float32)
        add_key_rows = lax.all_gather(points.astype(jnp.float32), "blk", axis=0, tiled=True).astype(
            jnp.bfloat16
        )
        fold_direction_rows = lax.all_gather(direction_now, "blk", axis=0, tiled=True)
        piece_rows = add_key_rows.shape[0]
        splits = piece_rows // row_count

        def scan_step(carry, operands):
            return (tile_add(carry, operands[0], operands[1], operands[2]), None)

        stacked = (
            add_key_rows.reshape(splits, row_count, add_key_rows.shape[1]),
            squared_norms(add_key_rows).reshape(splits, row_count),
            fold_direction_rows.reshape(splits, row_count, fold_direction_rows.shape[1]),
        )
        result, unused = lax.scan(scan_step, empty, stacked)
        image = (
            lax.psum_scatter(result, "col", scatter_dimension=0, tiled=True)
            + noise_level * direction_now
        )
        curvature = lax.psum(jnp.sum(direction_now * image, axis=0), ("blk", "col"))
        step_size = inner_now / curvature
        solution = solution + step_size * direction_now
        residual = residual - step_size * image
        if step_index + 1 < ITERS:
            scaled, inner_next = precondition(residual)
            direction_now = scaled + inner_next / inner_now * direction_now
            inner_now = inner_next
    return (factor, solution, residual)


def solution(mesh):
    return jax.shard_map(
        per_device,
        mesh=mesh,
        in_specs=(P(("blk", "col"), None), P(("blk", "col"), None), P()),
        out_specs=(P(("blk", "col"), None), P(("blk", "col"), None), P(("blk", "col"), None)),
        check_vma=False,
    )
```

profile of v0, /device:TPU:1, one launch (start us, length us, event | category | flops | bytes accessed | tf_op | source)
XLA Modules:
  0.0 2410.5 jit_solution(17141482593332180947)
XLA Ops:
  8.9 82.6 %all-reduce.14 = bf16[512,128]{1,0:T(8,128)(2,1)S(1)} all-reduce(f32[512,128]{1,0:T(8,128)S(1)} %fusion.57), channel_id=1, replica_groups=mesh['blk'=64,'col'=4] {'blk','col'}, use_global_device_ids=true, to_apply=%region_0.0 | all-reduce | flops 65536 | bytes 393216 | tf_op jit(solution)/shard_map/psum | solution.py:67
  92.1 11.7 cholesky.354
  103.9 9.8 custom-call.54
  114.3 11.7 cholesky.364
  129.2 4.4 while.53
  130.0 1.4 dynamic-slice.27
  132.1 1.4 dynamic-slice.27
  133.6 19.7 custom-call.55
  156.1 11.7 cholesky.381
  167.8 9.8 custom-call.56
  178.1 11.7 cholesky.391
  192.9 4.0 while.54
  193.5 1.4 bitcast_dynamic-update-slice_fusion.7
  195.5 1.4 bitcast_dynamic-update-slice_fusion.7
  196.9 19.7 custom-call.57
  218.0 2.0 fusion.240
  221.1 251.4 %all-reduce.13.cloned.1.call-done = (f32[512,512]{1,0:T(8,128)}, f32[512,32]{0,1:T(8,128)}) async-done(((f32[512,512]{1,0:T(8,128)}, f32[512,32]{0,1:T(8,128)}), (f32[512,512]{1,0:T(8,128)}, f32[512,32]{0,1:T(8,128)})) %all-reduce.13.cloned.1.call-update) | async-done | bytes 1114128 | tf_op jit(solution)/shard_map/psum | solution.py:73
  472.5 1.4 select_add_fusion
  474.5 11.7 cholesky.166
  486.4 9.8 custom-call.42
  496.9 11.7 cholesky.189
  509.9 10.0 custom-call.43
  520.5 11.7 cholesky.292
  533.0 9.8 custom-call.58
  543.4 11.7 cholesky.305
  558.7 10.4 while.55
  559.3 2.0 bitcast_dynamic-update-slice_fusion.8
  561.9 2.0 bitcast_dynamic-update-slice_fusion.8
  564.5 2.0 bitcast_dynamic-update-slice_fusion.8
  567.1 2.0 bitcast_dynamic-update-slice_fusion.8
  569.1 40.1 %custom-call.59 = f32[4,128,128]{1,2,0:T(8,128)S(1)} custom-call(f32[4,128,128]{2,1,0:T(8,128)} %get-tuple-element.393), custom_call_target="InvertDiagBlocksLowerTriangular" | custom-call | tf_op jit(solution)/shard_map/jit(_cho_solve)/triangular_solve | solution.py:82
  614.2 6.7 all_gather.17
  621.0 92.2 %all-gather.7.cloned.1.call-done = f32[8192,32]{0,1:T(8,128)} async-done(((f32[128,32]{0,1:T(8,128)}), f32[8192,32]{0,1:T(8,128)}) %all-gather.7.cloned.1.call-update) | async-done | bytes 1048592 | tf_op jit(solution)/shard_map/all_gather | solution.py:103
  713.2 3.6 copy.29
  716.7 116.0 %all-gather.5.cloned.1.call-done = bf16[8192,128]{1,0:T(8,128)(2,1)} async-done(((bf16[128,128]{1,0:T(8,128)(2,1)}), bf16[8192,128]{1,0:T(8,128)(2,1)}) %all-gather.5.cloned.1.call-update) | async-done | bytes 2097168 | tf_op jit(solution)/shard_map/all_gather | solution.py:100
  832.7 2.7 multiply_reduce_fusion
  835.5 144.7 %while.50 = (s32[]{:T(128)}, f32[512,32]{0,1:T(8,128)S(1)}, f32[512]{0:T(512)S(1)}, f32[64,128]{1,0:T(8,128)S(1)}, bf16[64,128,128]{2,1,0:T(8,128)(2,1)}, /*inde...) while((s32[]{:T(128)}, f32[512,32]{0,1:T(8,128)S(1)}, ...), condition=%wide.region_23.28_spmd.clone, body=%wide.region_22.27_spmd.clone.sunk | while | flops 42237952 | bytes 889451 | solution.py:115
  980.9 20.1 reduce-scatter.4.cloned.1.call-done
  1001.8 77.0 %all-reduce.2 = (f32[32]{0:T(128)S(1)}, f32[32]{0:T(128)S(1)}) all-reduce(f32[32]{0:T(128)S(1)} %get-tuple-element.431, f32[32]{0:T(128)S(1)} %get-tuple-element.430), channel_id=1, replica_groups=mesh['blk'=64,'col'=4] {'blk','col'}, use_global_device_ids=true, to_apply=%region_19.24 | all-reduce | flops 64 | bytes 512 | tf_op jit(solution)/shard_map/psum | solution.py:86
  1079.9 234.4 %all-reduce.9.cloned.1.call-done = f32[512,32]{0,1:T(8,128)} async-done(((f32[512,32]{0,1:T(8,128)}), f32[512,32]{0,1:T(8,128)}) %all-reduce.9.cloned.1.call-update) | async-done | bytes 65552 | tf_op jit(solution)/shard_map/psum | solution.py:81
  1320.8 74.4 %psum.83 = f32[32]{0:T(128)S(1)} all-reduce(f32[32]{0:T(128)S(1)} %get-tuple-element.537), channel_id=1, replica_groups=mesh['blk'=64,'col'=4] {'blk','col'}, use_global_device_ids=true, to_apply=%region_29.34 | all-reduce | flops 32 | bytes 256 | tf_op jit(solution)/shard_map/psum | solution.py:86
  1396.0 95.6 %all-gather.9.cloned.1.call-done = f32[8192,32]{0,1:T(8,128)} async-done(((f32[128,32]{0,1:T(8,128)}), f32[8192,32]{0,1:T(8,128)}) %all-gather.9.cloned.1.call-update) | async-done | bytes 1048592 | tf_op jit(solution)/shard_map/all_gather | solution.py:103
  1491.5 3.6 copy.30
  1495.1 144.7 %while.51 = (s32[]{:T(128)}, f32[512,32]{0,1:T(8,128)S(1)}, f32[512]{0:T(512)S(1)}, f32[64,128]{1,0:T(8,128)S(1)}, bf16[64,128,128]{2,1,0:T(8,128)(2,1)}, /*inde...) while((s32[]{:T(128)}, f32[512,32]{0,1:T(8,128)S(1)}, ...), condition=%wide.region_31.36_spmd.clone, body=%wide.region_30.35_spmd.clone.sunk | while | flops 42237952 | bytes 889451 | solution.py:115
  1507.4 1.2 convolution_add_fusion.7
  1511.9 1.2 convolution_add_fusion.7
  1516.5 1.2 convolution_add_fusion.7
  1525.5 1.2 convolution_add_fusion.7
  1530.0 1.2 convolution_add_fusion.7
  1543.6 1.2 convolution_add_fusion.7
  1548.1 1.2 convolution_add_fusion.7
  1561.7 1.2 convolution_add_fusion.7
  1566.2 1.2 convolution_add_fusion.7
  1575.2 1.2 convolution_add_fusion.7
  1640.5 21.1 reduce-scatter.6.cloned.1.call-done
  1662.4 77.3 %psum.84 = f32[32]{0:T(128)S(1)} all-reduce(f32[32]{0:T(128)S(1)} %multiply_reduce_fusion.7), channel_id=1, replica_groups=mesh['blk'=64,'col'=4] {'blk','col'}, use_global_device_ids=true, to_apply=%region_34.39 | all-reduce | flops 32 | bytes 256 | tf_op jit(solution)/shard_map/psum | solution.py:120
  1741.6 234.4 %all-reduce.11.cloned.1.call-done = f32[512,32]{0,1:T(8,128)} async-done(((f32[512,32]{0,1:T(8,128)}), f32[512,32]{0,1:T(8,128)}) %all-reduce.11.cloned.1.call-update) | async-done | bytes 65552 | tf_op jit(solution)/shard_map/psum | solution.py:81
  1982.4 74.4 %psum.86 = f32[32]{0:T(128)S(1)} all-reduce(f32[32]{0:T(128)S(1)} %get-tuple-element.539), channel_id=1, replica_groups=mesh['blk'=64,'col'=4] {'blk','col'}, use_global_device_ids=true, to_apply=%region_37.42 | all-reduce | flops 32 | bytes 256 | tf_op jit(solution)/shard_map/psum | solution.py:86
  2057.6 95.6 %all-gather.11.cloned.1.call-done = f32[8192,32]{0,1:T(8,128)} async-done(((f32[128,32]{0,1:T(8,128)}), f32[8192,32]{0,1:T(8,128)}) %all-gather.11.cloned.1.call-update) | async-done | bytes 1048592 | tf_op jit(solution)/shard_map/all_gather | solution.py:103
  2153.2 3.6 copy.31
  2156.8 144.7 %while.52 = (s32[]{:T(128)}, f32[512,32]{0,1:T(8,128)S(1)}, f32[512]{0:T(512)S(1)}, f32[64,128]{1,0:T(8,128)S(1)}, bf16[64,128,128]{2,1,0:T(8,128)(2,1)}, /*inde...) while((s32[]{:T(128)}, f32[512,32]{0,1:T(8,128)S(1)}, ...), condition=%wide.region_39.44_spmd.clone, body=%wide.region_38.43_spmd.clone.sunk | while | flops 42237952 | bytes 889451 | solution.py:115
  2302.1 21.1 reduce-scatter.8.cloned.1.call-done
  2324.8 77.0 %psum.87 = f32[32]{0:T(128)S(1)} all-reduce(f32[32]{0:T(128)S(1)} %multiply_reduce_fusion.5), channel_id=1, replica_groups=mesh['blk'=64,'col'=4] {'blk','col'}, use_global_device_ids=true, to_apply=%region_42.47 | all-reduce | flops 32 | bytes 256 | tf_op jit(solution)/shard_map/psum | solution.py:120
  2401.8 1.4 multiply_subtract_fusion
  (767 shorter events, 463.6 us)
Async XLA Ops:
  7.2 119.0 %copy-start.5 = (bf16[128,128]{1,0:T(8,128)(2,1)S(1)}, bf16[128,128]{1,0:T(8,128)(2,1)}, u32[]{:S(2)}) copy-start(bf16[128,128]{1,0:T(8,128)(2,1)} %param.16) | copy-start | bytes 98308
  7.2 465.3 %all-reduce.13.cloned.1.call-start = ((), (), s32[]{:S(2)}) async-start(), calls=%async_computation.12 | async-start | bytes 2228224 | tf_op jit(solution)/shard_map/psum | solution.py:73
  154.5 65.5 %copy-start.8 = (f32[128,32]{0,1:T(8,128)S(1)}, f32[128,32]{0,1:T(8,128)}, u32[]{:S(2)}) copy-start(f32[128,32]{0,1:T(8,128)} %param.17) | copy-start | bytes 49156
  221.1 492.1 %all-gather.7.cloned.1.call-start = ((), (), s32[]{:S(2)}) async-start(), calls=%async_computation.4 | async-start | bytes 1064960 | tf_op jit(solution)/shard_map/all_gather | solution.py:103
  472.5 1.8 copy-start
  474.5 134.7 %copy-start.9 = (f32[512,32]{0,1:T(8,128)S(1)}, f32[512,32]{0,1:T(8,128)}, u32[]{:S(2)}) copy-start(f32[512,32]{0,1:T(8,128)} %get-tuple-element.501) | copy-start | bytes 196612
  496.5 117.6 %copy-start.6 = (bf16[128,128]{1,0:T(8,128)(2,1)S(1)}, bf16[128,128]{1,0:T(8,128)(2,1)}, u32[]{:S(2)}) copy-start(bf16[128,128]{1,0:T(8,128)(2,1)} %param.16) | copy-start | bytes 98308
  613.3 219.4 %all-gather.5.cloned.1.call-start = ((), (), s32[]{:S(2)}) async-start(), calls=%async_computation.3 | async-start | bytes 2129920 | tf_op jit(solution)/shard_map/all_gather | solution.py:100
  614.1 386.8 %reduce-scatter.4.cloned.1.call-start = ((), (), s32[]{:S(2)}) async-start(), calls=%async_computation.5 | async-start | bytes 81920 | tf_op jit(solution)/shard_map/reduce_scatter | solution.py:117
  980.2 0.6 copy-start.1
  980.8 333.5 %all-reduce.9.cloned.1.call-start = ((), (), s32[]{:S(2)}) async-start(), calls=%async_computation.6 | async-start | bytes 131072 | tf_op jit(solution)/shard_map/psum | solution.py:81
  1079.9 411.7 %all-gather.9.cloned.1.call-start = ((), (), s32[]{:S(2)}) async-start(), calls=%async_computation.7 | async-start | bytes 1064960 | tf_op jit(solution)/shard_map/all_gather | solution.py:103
  1395.9 265.7 %reduce-scatter.6.cloned.1.call-start = ((), (), s32[]{:S(2)}) async-start(), calls=%async_computation.8 | async-start | bytes 81920 | tf_op jit(solution)/shard_map/reduce_scatter | solution.py:117
  1396.0 265.6 %copy-start.4 = (f32[128,32]{0,1:T(8,128)S(1)}, f32[128,32]{0,1:T(8,128)}, u32[]{:S(2)}) copy-start(f32[128,32]{0,1:T(8,128)} %multiply_add_fusion.4) | copy-start | bytes 49156
  1639.8 0.6 copy-start.2
  1640.5 335.5 %all-reduce.11.cloned.1.call-start = ((), (), s32[]{:S(2)}) async-start(), calls=%async_computation.9 | async-start | bytes 131072 | tf_op jit(solution)/shard_map/psum | solution.py:81
  1741.5 411.7 %all-gather.11.cloned.1.call-start = ((), (), s32[]{:S(2)}) async-start(), calls=%async_computation.10 | async-start | bytes 1064960 | tf_op jit(solution)/shard_map/all_gather | solution.py:103
  2057.5 265.7 %reduce-scatter.8.cloned.1.call-start = ((), (), s32[]{:S(2)}) async-start(), calls=%async_computation.11 | async-start | bytes 81920 | tf_op jit(solution)/shard_map/reduce_scatter | solution.py:117
  2057.6 265.6 %copy-start.7 = (f32[128,32]{0,1:T(8,128)S(1)}, f32[128,32]{0,1:T(8,128)}, u32[]{:S(2)}) copy-start(f32[128,32]{0,1:T(8,128)} %multiply_add_fusion.2) | copy-start | bytes 49156
  2301.4 0.6 copy-start.3
Sparse Core Ops, SparseCore 0:
  221.2 251.2 all-reduce.12
  613.5 99.6 all-gather.6
  717.3 115.3 all-gather.4
  981.0 19.9 reduce-scatter.3
  1080.0 234.2 all-reduce.8
  1396.0 95.4 all-gather.8
  1640.6 20.9 reduce-scatter.5
  1741.6 234.2 all-reduce.10
  2057.6 95.4 all-gather.10
  2302.2 20.9 reduce-scatter.7
where the time goes:
time: 2440 us; the launch traced here: 2410 us
  waiting for transfers between devices  1180 us (48%)
  blocking collectives  469 us (19%)
  matrix products  455 us (19%)
  other arithmetic  239 us (10%)
  local copies, waits for them, and re-layouts  35.5 us (1%)
    psum x2, waiting for transfers between devices, precondition(): projection = lax.psum(local_proj, ('blk', 'col'))  469 us
    all_gather x3, waiting for transfers between devices, per_device(): lax.all_gather(direction_now, 'blk', axis=0, tiled=True)  283 us
    psum x1, waiting for transfers between devices, per_device(): gram = lax.psum(local_gram, ('blk', 'col'))  251 us
    dot_general x192, matrix products, tile_add(): return total + jnp.dot(weights, direction_rows, precision=highest)  238 us
    psum x3, blocking collectives, precondition(): lax.psum(jnp.sum(residual_now * scaled, axis=0), ('blk', 'col'))  226 us
    dot_general x197, matrix products, kernel_block(): lax.dot_general(left_rows, right_rows, (((1,), (1,)), ((), ())), preferre...  187 us
    psum x2, blocking collectives, per_device(): curvature = lax.psum(jnp.sum(direction_now * image, axis=0), ('blk', 'col'))  154 us
    all_gather x1, waiting for transfers between devices, per_device(): lax.all_gather(points.astype(jnp.float32), 'blk', axis=0, tiled=True)  116 us
  transfers between devices with their start and end apart: 10, of which 10 were waited for; matrix products, arithmetic and copies ran while one was open for 0% of the time, Pallas kernels for 0%

commit v1 on v0

--- a/solution.py
+++ b/solution.py
@@ -97,9 +97,12 @@
     direction_now, inner_now = precondition(residual)
     for step_index in range(ITERS):
         empty = jnp.zeros((own_block.shape[0], direction_now.shape[1]), jnp.float32)
-        add_key_rows = lax.all_gather(points.astype(jnp.float32), "blk", axis=0, tiled=True).astype(
-            jnp.bfloat16
-        )
+        add_key_rows = jnp.concatenate(
+            lax.all_to_all(
+                jnp.stack(lax.axis_size("blk") * [points.astype(jnp.float32)], axis=0), "blk", 0, 0
+            ),
+            0,
+        ).astype(jnp.bfloat16)
         fold_direction_rows = lax.all_gather(direction_now, "blk", axis=0, tiled=True)
         piece_rows = add_key_rows.shape[0]
         splits = piece_rows // row_count

time: 2440 us -> 2340 us (0.959)
  waiting for transfers between devices: 1180 us -> 1070 us
    all_gather x1 -> x0, waiting for transfers between devices: 116 us -> none  [per_device(): lax.all_gather(points.astype(jnp.float32), 'blk', axis=0, tiled=True)]
  transfers between devices with their start and end apart: 10 -> 10, of which waited for: 10 -> 9; matrix products, arithmetic and copies ran while one was open for 0% -> 6% of each run, Pallas kernels for 0% -> 0%
where the time goes in v1:
time: 2340 us; the launch traced here: 2310 us
  waiting for transfers between devices  1070 us (46%)
  blocking collectives  469 us (20%)
  matrix products  455 us (19%)
  other arithmetic  240 us (10%)
  local copies, waits for them, and re-layouts  37.3 us (2%)
    psum x2, waiting for transfers between devices, precondition(): projection = lax.psum(local_proj, ('blk', 'col'))  469 us
    all_gather x3, waiting for transfers between devices, per_device(): lax.all_gather(direction_now, 'blk', axis=0, tiled=True)  284 us
    psum x1, waiting for transfers between devices, per_device(): gram = lax.psum(local_gram, ('blk', 'col'))  254 us
    dot_general x192, matrix products, tile_add(): return total + jnp.dot(weights, direction_rows, precision=highest)  238 us
    psum x3, blocking collectives, precondition(): lax.psum(jnp.sum(residual_now * scaled, axis=0), ('blk', 'col'))  226 us
    dot_general x197, matrix products, kernel_block(): lax.dot_general(left_rows, right_rows, (((1,), (1,)), ((), ())), preferre...  187 us
    psum x2, blocking collectives, per_device(): curvature = lax.psum(jnp.sum(direction_now * image, axis=0), ('blk', 'col'))  154 us
    psum x1, blocking collectives, per_device(): picked = lax.psum(local_pick, ('blk', 'col')).astype(jnp.bfloat16)  82.6 us
  transfers between devices with their start and end apart: 10, of which 9 were waited for; matrix products, arithmetic and copies ran while one was open for 6% of the time, Pallas kernels for 0%

profile of v1, /device:TPU:1, one launch (start us, length us, event | category | flops | bytes accessed | tf_op | source)
XLA Modules:
  0.0 2307.6 jit_solution(2242038414064146537)
XLA Ops:
  9.8 82.6 %all-reduce.14 = bf16[512,128]{1,0:T(8,128)(2,1)S(1)} all-reduce(f32[512,128]{1,0:T(8,128)S(1)} %fusion.57), channel_id=1, replica_groups=mesh['blk'=64,'col'=4] {'blk','col'}, use_global_device_ids=true, to_apply=%region_0.0 | all-reduce | flops 65536 | bytes 393216 | tf_op jit(solution)/shard_map/psum | solution.py:67
  92.9 11.7 cholesky.354
  104.8 9.8 custom-call.54
  115.2 11.7 cholesky.364
  130.0 4.4 while.53
  130.7 1.4 dynamic-slice.27
  132.9 1.4 dynamic-slice.27
  134.4 19.7 custom-call.55
  157.4 11.7 cholesky.381
  169.2 9.8 custom-call.56
  179.5 12.1 cholesky.391
  194.2 4.0 while.54
  194.8 1.4 bitcast_dynamic-update-slice_fusion.7
  196.8 1.4 bitcast_dynamic-update-slice_fusion.7
  198.2 19.7 custom-call.57
  218.7 2.0 fusion.240
  221.8 1.9 stack.2
  223.6 6.7 all-to-all-start
  230.4 254.5 %all-reduce.13.cloned.1.call-done = (f32[512,512]{1,0:T(8,128)}, f32[512,32]{0,1:T(8,128)}) async-done(((f32[512,512]{1,0:T(8,128)}, f32[512,32]{0,1:T(8,128)}), (f32[512,512]{1,0:T(8,128)}, f32[512,32]{0,1:T(8,128)})) %all-reduce.13.cloned.1.call-update) | async-done | bytes 1114128 | tf_op jit(solution)/shard_map/psum | solution.py:73
  484.9 1.4 select_add_fusion
  486.9 11.7 cholesky.166
  498.8 9.8 custom-call.42
  509.3 11.7 cholesky.189
  521.0 10.0 custom-call.43
  531.7 11.7 cholesky.292
  543.4 9.8 custom-call.58
  553.8 11.7 cholesky.305
  571.1 10.4 while.55
  571.7 2.0 bitcast_dynamic-update-slice_fusion.8
  574.3 2.0 bitcast_dynamic-update-slice_fusion.8
  576.9 2.0 bitcast_dynamic-update-slice_fusion.8
  579.5 2.0 bitcast_dynamic-update-slice_fusion.8
  581.5 40.1 %custom-call.59 = f32[4,128,128]{1,2,0:T(8,128)S(1)} custom-call(f32[4,128,128]{2,1,0:T(8,128)} %get-tuple-element.393), custom_call_target="InvertDiagBlocksLowerTriangular" | custom-call | tf_op jit(solution)/shard_map/jit(_cho_solve)/triangular_solve | solution.py:82
  625.8 6.7 all_gather.12
  632.6 92.9 %all-gather.4.cloned.1.call-done = f32[8192,32]{0,1:T(8,128)} async-done(((f32[128,32]{0,1:T(8,128)}), f32[8192,32]{0,1:T(8,128)}) %all-gather.4.cloned.1.call-update) | async-done | bytes 1048592 | tf_op jit(solution)/shard_map/all_gather | solution.py:106
  725.5 3.6 copy.29
  729.1 2.7 multiply_reduce_fusion
  731.9 144.7 %while.50 = (s32[]{:T(128)}, f32[512,32]{0,1:T(8,128)S(1)}, f32[512]{0:T(512)S(1)}, f32[64,128]{1,0:T(8,128)S(1)}, bf16[64,128,128]{2,1,0:T(8,128)(2,1)}, /*inde...) while((s32[]{:T(128)}, f32[512,32]{0,1:T(8,128)S(1)}, ...), condition=%wide.region_23.28_spmd.clone, body=%wide.region_22.27_spmd.clone.sunk | while | flops 42237952 | bytes 888443 | solution.py:118
  735.1 1.2 convolution_add_fusion.6
  748.7 1.2 convolution_add_fusion.6
  766.8 1.2 convolution_add_fusion.6
  784.9 1.2 convolution_add_fusion.6
  798.4 1.2 convolution_add_fusion.6
  803.0 1.2 convolution_add_fusion.6
  816.5 1.2 convolution_add_fusion.6
  877.3 21.1 reduce-scatter.4.cloned.1.call-done
  899.2 77.0 %all-reduce.2 = (f32[32]{0:T(128)S(1)}, f32[32]{0:T(128)S(1)}) all-reduce(f32[32]{0:T(128)S(1)} %get-tuple-element.431, f32[32]{0:T(128)S(1)} %get-tuple-element.430), channel_id=1, replica_groups=mesh['blk'=64,'col'=4] {'blk','col'}, use_global_device_ids=true, to_apply=%region_19.24 | all-reduce | flops 64 | bytes 512 | tf_op jit(solution)/shard_map/psum | solution.py:86
  977.4 234.3 %all-reduce.9.cloned.1.call-done = f32[512,32]{0,1:T(8,128)} async-done(((f32[512,32]{0,1:T(8,128)}), f32[512,32]{0,1:T(8,128)}) %all-reduce.9.cloned.1.call-update) | async-done | bytes 65552 | tf_op jit(solution)/shard_map/psum | solution.py:81
  1218.1 74.4 %psum.83 = f32[32]{0:T(128)S(1)} all-reduce(f32[32]{0:T(128)S(1)} %get-tuple-element.537), channel_id=1, replica_groups=mesh['blk'=64,'col'=4] {'blk','col'}, use_global_device_ids=true, to_apply=%region_29.34 | all-reduce | flops 32 | bytes 256 | tf_op jit(solution)/shard_map/psum | solution.py:86
  1293.3 95.6 %all-gather.6.cloned.1.call-done = f32[8192,32]{0,1:T(8,128)} async-done(((f32[128,32]{0,1:T(8,128)}), f32[8192,32]{0,1:T(8,128)}) %all-gather.6.cloned.1.call-update) | async-done | bytes 1048592 | tf_op jit(solution)/shard_map/all_gather | solution.py:106
  1388.9 3.6 copy.30
  1392.5 144.7 %while.51 = (s32[]{:T(128)}, f32[512,32]{0,1:T(8,128)S(1)}, f32[512]{0:T(512)S(1)}, f32[64,128]{1,0:T(8,128)S(1)}, bf16[64,128,128]{2,1,0:T(8,128)(2,1)}, /*inde...) while((s32[]{:T(128)}, f32[512,32]{0,1:T(8,128)S(1)}, ...), condition=%wide.region_31.36_spmd.clone, body=%wide.region_30.35_spmd.clone.sunk | while | flops 42237952 | bytes 888443 | solution.py:118
  1398.0 1.2 convolution_add_fusion.7
  1537.9 21.1 reduce-scatter.6.cloned.1.call-done
  1559.8 77.3 %psum.84 = f32[32]{0:T(128)S(1)} all-reduce(f32[32]{0:T(128)S(1)} %multiply_reduce_fusion.7), channel_id=1, replica_groups=mesh['blk'=64,'col'=4] {'blk','col'}, use_global_device_ids=true, to_apply=%region_34.39 | all-reduce | flops 32 | bytes 256 | tf_op jit(solution)/shard_map/psum | solution.py:123
  1638.9 234.4 %all-reduce.11.cloned.1.call-done = f32[512,32]{0,1:T(8,128)} async-done(((f32[512,32]{0,1:T(8,128)}), f32[512,32]{0,1:T(8,128)}) %all-reduce.11.cloned.1.call-update) | async-done | bytes 65552 | tf_op jit(solution)/shard_map/psum | solution.py:81
  1879.8 74.4 %psum.86 = f32[32]{0:T(128)S(1)} all-reduce(f32[32]{0:T(128)S(1)} %get-tuple-element.539), channel_id=1, replica_groups=mesh['blk'=64,'col'=4] {'blk','col'}, use_global_device_ids=true, to_apply=%region_37.42 | all-reduce | flops 32 | bytes 256 | tf_op jit(solution)/shard_map/psum | solution.py:86
  1955.0 95.6 %all-gather.8.cloned.1.call-done = f32[8192,32]{0,1:T(8,128)} async-done(((f32[128,32]{0,1:T(8,128)}), f32[8192,32]{0,1:T(8,128)}) %all-gather.8.cloned.1.call-update) | async-done | bytes 1048592 | tf_op jit(solution)/shard_map/all_gather | solution.py:106
  2050.5 3.6 copy.31
  2054.1 144.7 %while.52 = (s32[]{:T(128)}, f32[512,32]{0,1:T(8,128)S(1)}, f32[512]{0:T(512)S(1)}, f32[64,128]{1,0:T(8,128)S(1)}, bf16[64,128,128]{2,1,0:T(8,128)(2,1)}, /*inde...) while((s32[]{:T(128)}, f32[512,32]{0,1:T(8,128)S(1)}, ...), condition=%wide.region_39.44_spmd.clone, body=%wide.region_38.43_spmd.clone.sunk | while | flops 42237952 | bytes 888443 | solution.py:118
  2057.4 1.2 convolution_add_fusion.8
  2199.5 21.1 reduce-scatter.8.cloned.1.call-done
  2222.2 77.0 %psum.87 = f32[32]{0:T(128)S(1)} all-reduce(f32[32]{0:T(128)S(1)} %multiply_reduce_fusion.5), channel_id=1, replica_groups=mesh['blk'=64,'col'=4] {'blk','col'}, use_global_device_ids=true, to_apply=%region_42.47 | all-reduce | flops 32 | bytes 256 | tf_op jit(solution)/shard_map/psum | solution.py:123
  2299.2 1.4 multiply_subtract_fusion
  (765 shorter events, 464.5 us)
Async XLA Ops:
  7.2 120.1 %copy-start.5 = (bf16[128,128]{1,0:T(8,128)(2,1)S(1)}, bf16[128,128]{1,0:T(8,128)(2,1)}, u32[]{:S(2)}) copy-start(bf16[128,128]{1,0:T(8,128)(2,1)} %param.16) | copy-start | bytes 98308
  7.2 477.7 %all-reduce.13.cloned.1.call-start = ((), (), s32[]{:S(2)}) async-start(), calls=%async_computation.12 | async-start | bytes 2228224 | tf_op jit(solution)/shard_map/psum | solution.py:73
  155.4 65.4 %copy-start.7 = (f32[128,32]{0,1:T(8,128)S(1)}, f32[128,32]{0,1:T(8,128)}, u32[]{:S(2)}) copy-start(f32[128,32]{0,1:T(8,128)} %param.17) | copy-start | bytes 49156
  223.6 505.5 %all-to-all-start = ((bf16[64,128,128]{2,1,0:T(8,128)(2,1)}), bf16[64,128,128]{2,1,0:T(8,128)(2,1)}, u32[]{:S(2)}, u32[]{:S(2)}) async-start(bf16[64,128,128]{2,1,0:T(8,128)(2,1)} %stack.2), calls=%async_computation | async-start | bytes 4194304 | tf_op jit(solution)/shard_map/all_to_all | solution.py:101
  230.4 495.1 %all-gather.4.cloned.1.call-start = ((), (), s32[]{:S(2)}) async-start(), calls=%async_computation.4 | async-start | bytes 1064960 | tf_op jit(solution)/shard_map/all_gather | solution.py:106
  484.9 1.8 copy-start
  486.9 134.7 %copy-start.8 = (f32[512,32]{0,1:T(8,128)S(1)}, f32[512,32]{0,1:T(8,128)}, u32[]{:S(2)}) copy-start(f32[512,32]{0,1:T(8,128)} %get-tuple-element.501) | copy-start | bytes 196612
  625.7 272.6 %reduce-scatter.4.cloned.1.call-start = ((), (), s32[]{:S(2)}) async-start(), calls=%async_computation.5 | async-start | bytes 81920 | tf_op jit(solution)/shard_map/reduce_scatter | solution.py:120
  876.6 0.6 copy-start.1
  877.2 334.5 %all-reduce.9.cloned.1.call-start = ((), (), s32[]{:S(2)}) async-start(), calls=%async_computation.6 | async-start | bytes 131072 | tf_op jit(solution)/shard_map/psum | solution.py:81
  977.3 411.6 %all-gather.6.cloned.1.call-start = ((), (), s32[]{:S(2)}) async-start(), calls=%async_computation.7 | async-start | bytes 1064960 | tf_op jit(solution)/shard_map/all_gather | solution.py:106
  1293.3 265.7 %reduce-scatter.6.cloned.1.call-start = ((), (), s32[]{:S(2)}) async-start(), calls=%async_computation.8 | async-start | bytes 81920 | tf_op jit(solution)/shard_map/reduce_scatter | solution.py:120
  1293.3 265.6 %copy-start.4 = (f32[128,32]{0,1:T(8,128)S(1)}, f32[128,32]{0,1:T(8,128)}, u32[]{:S(2)}) copy-start(f32[128,32]{0,1:T(8,128)} %multiply_add_fusion.4) | copy-start | bytes 49156
  1537.2 0.6 copy-start.2
  1537.8 335.5 %all-reduce.11.cloned.1.call-start = ((), (), s32[]{:S(2)}) async-start(), calls=%async_computation.9 | async-start | bytes 131072 | tf_op jit(solution)/shard_map/psum | solution.py:81
  1638.9 411.6 %all-gather.8.cloned.1.call-start = ((), (), s32[]{:S(2)}) async-start(), calls=%async_computation.10 | async-start | bytes 1064960 | tf_op jit(solution)/shard_map/all_gather | solution.py:106
  1954.9 265.7 %reduce-scatter.8.cloned.1.call-start = ((), (), s32[]{:S(2)}) async-start(), calls=%async_computation.11 | async-start | bytes 81920 | tf_op jit(solution)/shard_map/reduce_scatter | solution.py:120
  1955.0 265.6 %copy-start.6 = (f32[128,32]{0,1:T(8,128)S(1)}, f32[128,32]{0,1:T(8,128)}, u32[]{:S(2)}) copy-start(f32[128,32]{0,1:T(8,128)} %multiply_add_fusion.2) | copy-start | bytes 49156
  2198.8 0.6 copy-start.3
Sparse Core Ops, SparseCore 0:
  221.9 262.9 all-reduce.12
  625.8 99.6 all-gather.3
  877.3 20.9 reduce-scatter.3
  977.4 234.2 all-reduce.8
  1293.4 95.4 all-gather.5
  1538.0 20.9 reduce-scatter.5
  1639.0 234.2 all-reduce.10
  1955.0 95.4 all-gather.7
  2199.6 20.9 reduce-scatter.7
